TPU v7x, 1024 devices: a whole 4x8x16 slice. The times are simulated.
1024 devices in a mesh: occ: 64 (over x, z), vir: 16 (over y, core).
Axes of the slice: x: 4, y: 8, z: 16, core: 2. Of those that a mesh axis runs over, the one named last changes fastest.
Arguments:
- amps: float32 [8192, 16, 1024], P('occ', 'vir'), may hold values from -6 to 6
- resid: float32 [8192, 16, 1024], P('occ', 'vir'), may hold values from -6 to 6
- ints: float32 [16, 1024, 1024], P('vir', 'occ'), may hold values from -0.5 to 0.5
- tasks: int32 [16], replicated, may hold values from 0 to 15
- pair_tiles: int32 [16, 2], replicated, may hold values from 0 to 18
- irreps: int32 [19, 32], replicated, may hold values from 0 to 7
Outputs:
- updated: float32 [8192, 16, 1024], P('occ', 'vir')
All inputs are finite; a program needn't handle non-finite values.
Results may differ from a plain program's by a relative error of at most 0.0003.
Values sent between devices are 32-bit elements; how exact they have to be, the bound alone decides.
A program may use at most 32 MiB of HBM per device.

v0:
```python
import jax
import jax.numpy as jnp
from jax import lax
from jax.sharding import PartitionSpec as P


def tile_irreps(tile_pair, irreps):
    tile_count = irreps.shape[0]
    tile_ids = jnp.arange(tile_count, dtype=jnp.int32)
    first_row = jnp.sum(jnp.where(tile_ids[:, None] == tile_pair[0], irreps, 0), axis=0)
    second_row = jnp.sum(jnp.where(tile_ids[:, None] == tile_pair[1], irreps, 0), axis=0)
    return jnp.bitwise_xor(first_row[:, None], second_row[None, :]).reshape(-1)


def contract(left, right):
    return lax.dot_general(
        left,
        right,
        (((1,), (1,)), ((), ())),
        precision=lax.Precision.HIGHEST,
        preferred_element_type=jnp.float32,
    )


def shards(amps, resid, ints, tasks, pair_tiles, irreps):
    own_tile = lax.axis_index("vir")
    cd_tile = lax.dynamic_index_in_dim(tasks, own_tile, 0, keepdims=False)
    ab_irrep = tile_irreps(
        lax.dynamic_index_in_dim(pair_tiles, own_tile, 0, keepdims=False), irreps
    )
    cd_irrep = tile_irreps(lax.dynamic_index_in_dim(pair_tiles, cd_tile, 0, keepdims=False), irreps)
    spread = lax.all_to_all(amps, "vir", split_axis=0, concat_axis=1, tiled=True)
    picked = jnp.take(spread, tasks, axis=1)
    returned = lax.all_to_all(picked, "vir", split_axis=1, concat_axis=0, tiled=True)
    chosen = returned[:, 0, :]
    effective = jnp.where(
        ab_irrep[:, None] == cd_irrep[None, :],
        lax.all_gather(ints, "occ", axis=1, tiled=True)[0],
        0.0,
    )
    ladder = contract(chosen, effective)
    return resid + ladder[:, None, :]


def solution(mesh):
    in_specs = (P("occ", "vir", None), P("occ", "vir", None), P("vir", "occ", None), P(), P(), P())
    out_specs = P("occ", "vir", None)
    return jax.shard_map(shards, mesh=mesh, in_specs=in_specs, out_specs=out_specs, check_vma=False)
```

profile of v0, /device:TPU:56, one launch (start us, length us, event | category | flops | bytes accessed | tf_op | source)
XLA Modules:
  0.0 186.2 jit_solution(10551727526977922929)
XLA Ops:
  6.5 0.7 all-gather.2.cloned.1.call-update
  7.3 15.9 %all-to-all-start = ((f32[128,1,1024]{2,1,0:T(1,128)}), f32[128,1,1024]{2,1,0:T(1,128)S(1)}, u32[]{:S(2)}, u32[]{:S(2)}) async-start(f32[128,1,1024]{2,1,0:T(1,128)} %param.6), calls=%async_computation | async-start | bytes 1048576 | tf_op jit(solution)/shard_map/all_to_all | solution.py:32
  23.1 1.2 dynamic_slice.12
  26.3 0.8 constant_dynamic-slice_fusion
  27.1 0.7 compare_select_fusion
  27.8 0.6 fusion.15
  28.4 0.7 compare_and_fusion
  29.1 7.7 %all-to-all-done = f32[128,1,1024]{2,1,0:T(1,128)S(1)} async-done(((f32[128,1,1024]{2,1,0:T(1,128)}), f32[128,1,1024]{2,1,0:T(1,128)S(1)}, u32[]{:S(2)}, u32[]{:S(2)}) %all-to-all-start) | async-done | bytes 524320 | tf_op jit(solution)/shard_map/all_to_all | solution.py:32
  36.8 0.1 copy.12
  36.9 0.6 gather_fusion
  37.5 0.9 select_bitcast_fusion
  38.4 6.5 %all-to-all-start.1 = ((f32[8,16,1024]{2,0,1:T(8,128)}), f32[8,16,1024]{2,0,1:T(8,128)S(1)}, u32[]{:S(2)}, u32[]{:S(2)}) async-start(f32[8,16,1024]{2,0,1:T(8,128)} %select_bitcast_fusion), calls=%async_computation.1 | async-start | bytes 1048576 | tf_op jit(solution)/shard_map/all_to_all | solution.py:34
  44.9 0.7 iota_compare_fusion
  45.6 0.6 iota_compare_fusion.1
  46.2 0.6 iota_compare_fusion.2
  46.7 0.6 iota_compare_fusion.3
  47.3 0.1 select_reduce_fusion.3
  47.4 0.1 broadcast_xor_fusion.1
  47.5 0.1 xor.43
  47.7 0.1 xor.47
  47.7 10.2 %all-to-all-done.1 = f32[8,16,1024]{2,0,1:T(8,128)S(1)} async-done(((f32[8,16,1024]{2,0,1:T(8,128)}), f32[8,16,1024]{2,0,1:T(8,128)S(1)}, u32[]{:S(2)}, u32[]{:S(2)}) %all-to-all-start.1) | async-done | bytes 524320 | tf_op jit(solution)/shard_map/all_to_all | solution.py:34
  57.9 113.5 %all-gather.2.cloned.1.call-done = f32[1,1024,1024]{2,1,0:T(8,128)} async-done(((f32[1,16,1024]{2,1,0:T(8,128)}), f32[1,1024,1024]{2,1,0:T(8,128)}) %all-gather.2.cloned.1.call-update) | async-done | bytes 4194320 | tf_op jit(solution)/shard_map/all_gather | solution.py:38
  171.4 6.6 %fusion.10 = f32[128,1,1024]{2,0,1:T(8,128)S(1)} fusion(f32[1,1024,1024]{2,1,0:T(8,128)} %all-gather.2.cloned.1.call-done, s32[1024]{0:T(1024)S(1)} %xor.47, s32[1024]{0:T(1024)S(1)} %xor.43, f32[8,16,1024]{2,0,1:T(8,128)S(1)} %all-to-all-done.1, f32[128,1,1024]{2,1,0:T(1,128)S(1)} %copy-done), kind=kOutput, calls=%fused_computation.9 | convolution fusion | flops 1612840960 | bytes 5775360 | tf_op jit(solution)/shard_map/dot_general | solution.py:16
  178.0 1.3 copy.8
  (7 shorter events, 0.1 us)
Async XLA Ops:
  6.5 40.8 %copy-start.1 = (s32[19,32]{1,0:T(8,128)S(1)}, s32[19,32]{1,0:T(8,128)}, u32[]{:S(2)}) copy-start(s32[19,32]{1,0:T(8,128)} %param.11) | copy-start | bytes 7300
  6.5 164.9 %copy-start = (f32[128,1,1024]{2,1,0:T(1,128)S(1)}, f32[128,1,1024]{2,1,0:T(1,128)}, u32[]{:S(2)}) copy-start(f32[128,1,1024]{2,1,0:T(1,128)} %param.7) | copy-start | bytes 1572868
  6.5 164.9 %all-gather.2.cloned.1.call-start = ((), (), s32[]{:S(2)}) async-start(), calls=%async_computation.2 | async-start | bytes 4259840 | tf_op jit(solution)/shard_map/all_gather | solution.py:38
  7.3 29.5 %all-to-all-start = ((f32[128,1,1024]{2,1,0:T(1,128)}), f32[128,1,1024]{2,1,0:T(1,128)S(1)}, u32[]{:S(2)}, u32[]{:S(2)}) async-start(f32[128,1,1024]{2,1,0:T(1,128)} %param.6), calls=%async_computation | async-start | bytes 1048576 | tf_op jit(solution)/shard_map/all_to_all | solution.py:32
  38.4 19.5 %all-to-all-start.1 = ((f32[8,16,1024]{2,0,1:T(8,128)}), f32[8,16,1024]{2,0,1:T(8,128)S(1)}, u32[]{:S(2)}, u32[]{:S(2)}) async-start(f32[8,16,1024]{2,0,1:T(8,128)} %select_bitcast_fusion), calls=%async_computation.1 | async-start | bytes 1048576 | tf_op jit(solution)/shard_map/all_to_all | solution.py:34
Sparse Core Ops, SparseCore 0:
  11.4 159.9 all-gather.1
where the time goes:
time: 187 us; the launch traced here: 186 us
  waiting for transfers between devices  132 us (71%)
  starting transfers between devices  22.3 us (12%)
  between operations  15.4 us (8%)
  matrix products  6.62 us (4%)
  other arithmetic  4.9 us (3%)
  local copies, waits for them, and re-layouts  4.83 us (3%)
    all_gather x1, waiting for transfers between devices, shards(): lax.all_gather(ints, 'occ', axis=1, tiled=True)[0]  114 us
    all_to_all x1, starting transfers between devices, shards(): lax.all_to_all(amps, 'vir', split_axis=0, concat_axis=1, tiled=True)  15.9 us
    all_to_all x1, waiting for transfers between devices, shards(): lax.all_to_all(picked, 'vir', split_axis=1, concat_axis=0, tiled=True)  10.2 us
    all_to_all x1, waiting for transfers between devices, shards(): lax.all_to_all(amps, 'vir', split_axis=0, concat_axis=1, tiled=True)  7.73 us
    dot_general x1, matrix products, contract(): lax.dot_general(left, right, (((1,), (1,)), ((), ())), precision=lax.Prec...  6.62 us
    all_to_all x1, starting transfers between devices, shards(): lax.all_to_all(picked, 'vir', split_axis=1, concat_axis=0, tiled=True)  6.48 us
  transfers between devices with their start and end apart: 3, of which 3 were waited for; matrix products, arithmetic and copies ran while one was open for 5% of the time, Pallas kernels for 0%

commit v1 on v0

v1 whole, which is shorter than its diff:
```python
import jax
import jax.numpy as jnp
from jax import lax
from jax.experimental import pallas as pl
from jax.experimental.pallas import tpu as pltpu
from jax.sharding import PartitionSpec as P

MESH = pl.DeviceIdType.MESH
X, Z, V = 4, 16, 16
SHARDS = X * Z
ROWS = 16
TILE = 32
COLS = 1024
BLOCKS = COLS // 128
NA = 3
WA = NA * 128
WB = COLS - WA
OCC = 128
SHARE = OCC // V
HALF = COLS // 2
FWD, BWD = Z // 2, Z // 2 - 1


def kernel(
    tasks, pairs, irr, amps, resid, ints, out,
    raw, ehi, elo, whole, sent0, sent1, spread0, spread1, picked, abuf, aa, base, col_key, cd_key,
    s_loc, s_a, s_b, s_y, r_ax, r_af, r_ab, r_bf, r_bb, r_bx, r_y1, r_y2,
):
    occ, vir = lax.axis_index("occ"), lax.axis_index("vir")
    x, z = occ // Z, occ % Z
    sign = 1 - 2 * (vir % 2)
    xf, xb = (x + sign + X) % X, (x - sign + X) % X
    xo = (x + 2) % X
    zf, zb = (z + sign + Z) % Z, (z - sign + Z) % Z
    to_xf, to_xb = (xf * Z + z, vir), (xb * Z + z, vir)
    to_zf, to_zb = (x * Z + zf, vir), (x * Z + zb, vir)

    load_amps = pltpu.make_async_copy(amps, whole, s_loc.at[1])
    load_amps.start()
    load_ints = pltpu.make_async_copy(ints, raw.at[occ], s_loc.at[0])
    load_ints.start()
    load_resid = pltpu.make_async_copy(resid, base, s_loc.at[2])
    load_resid.start()

    barrier = pltpu.get_barrier_semaphore()
    for who in (to_xf, to_xb, to_zf, to_zb):
        pl.semaphore_signal(barrier, inc=1, device_id=who, device_id_type=MESH)

    def greet(m, _):
        pl.semaphore_signal(barrier, inc=1, device_id=(occ, (vir + m) % V), device_id_type=MESH)
        return 0

    lax.fori_loop(1, V, greet, 0)

    tile_a, tile_b = pairs[0, vir], pairs[1, vir]
    task = tasks[vir]
    cd_a, cd_b = pairs[0, task], pairs[1, task]
    sub = lax.broadcasted_iota(jnp.int32, (ROWS, 128), 0)
    for par in range(2):
        key = jnp.zeros((ROWS, 128), jnp.int32)
        for j in range(ROWS):
            key = jnp.where(sub == j, irr[tile_b, par * ROWS + j], key)
        col_key[par] = key
    lane = lax.broadcasted_iota(jnp.int32, (1, 128), 1)
    minor = jnp.zeros((1, 128), jnp.int32)
    for j in range(TILE):
        minor = jnp.where(lane % TILE == j, irr[cd_b, j], minor)
    for b in range(BLOCKS):
        major = jnp.zeros((1, 128), jnp.int32)
        for j in range(4):
            major = jnp.where(lane // TILE == j, irr[cd_a, 4 * b + j], major)
        cd_key[:, 128 * b : 128 * b + 128] = major ^ minor

    sent, spread = (sent0, sent1), (spread0, spread1)
    load_amps.wait()

    def arrange(j, _):
        for b in range(BLOCKS):
            block = whole[pl.ds(SHARE * BLOCKS * j + b, SHARE, stride=BLOCKS), :]
            col = 128 * b % HALF
            sent[128 * b // HALF][j, :, col : col + 128] = block
        return 0

    lax.fori_loop(0, V, arrange, 0)
    load_ints.wait()
    pl.semaphore_wait(barrier, V + 3)

    def peer_at(i):
        return (vir + V // 2 + ((i + 1) // 2) * (1 - 2 * (i % 2)) + V) % V

    def spread_half(h):
        def send(i, _):
            peer = peer_at(i)
            pltpu.make_async_remote_copy(
                sent[h].at[peer], spread[h].at[vir],
                s_y.at[0, h], r_y1.at[h], device_id=(occ, peer), device_id_type=MESH,
            ).start()
            return 0

        lax.fori_loop(0, V - 1, send, 0)

    own_rows = pl.ds(pl.multiple_of(SHARE * vir, SHARE), SHARE)

    def return_half(h):
        many = spread[h].at[pl.ds(0, V - 1)]
        pltpu.make_async_copy(many, many, r_y1.at[h]).wait()
        for k in range(V):
            picked[h, k] = spread[h][tasks[k]]
        abuf[h, own_rows] = picked[h, vir]

        def send(i, _):
            peer = peer_at(i)
            pltpu.make_async_remote_copy(
                picked.at[h, peer], abuf.at[h, own_rows],
                s_y.at[1, h], r_y2.at[h], device_id=(occ, peer), device_id_type=MESH,
            ).start()
            return 0

        lax.fori_loop(0, V - 1, send, 0)

    def a_part(xx, zz):
        return raw.at[xx * Z + zz, :, pl.ds(0, WA)]

    def b_part(xx, zz):
        return raw.at[xx * Z + zz, :, pl.ds(WA, WB)]

    def push(part, send_sem, recv_sem, who):
        return pltpu.make_async_remote_copy(
            part, part, send_sem, recv_sem, device_id=who, device_id_type=MESH
        )

    def a_push(xx, zz, recv_sem, who):
        push(a_part(xx, zz), s_a.at[0], recv_sem, who).start()

    def b_push(xx, zz, recv_sem, who):
        push(b_part(xx, zz), s_b.at[0], recv_sem, who).start()

    def a_wait(xx, zz, recv_sem):
        push(a_part(xx, zz), s_a.at[0], recv_sem, to_xf).wait_recv()

    def b_wait(xx, zz, recv_sem):
        push(b_part(xx, zz), s_b.at[0], recv_sem, to_xf).wait_recv()

    xs = (x, xb, xf, xo)

    def prepare(xx, zz, first, last):
        shard = xx * Z + zz
        key = col_key[shard % 2] ^ irr[tile_a, shard // 2]
        rows = pl.ds(pl.multiple_of(shard * ROWS, ROWS), ROWS)
        cols = slice(128 * first, 128 * last)
        keys = jnp.concatenate([key] * (last - first), axis=1)
        value = jnp.where(keys == cd_key[:, cols], raw[shard, :, cols], 0.0)
        high = value.astype(jnp.bfloat16)
        ehi[rows, cols] = high
        elo[rows, cols] = (value - high.astype(jnp.float32)).astype(jnp.bfloat16)

    b_push(x, z, r_bf.at[0], to_zf)
    b_push(x, z, r_bb.at[0], to_zb)
    a_push(x, z, r_ax.at[0], to_xf)
    a_push(x, z, r_ax.at[1], to_xb)
    a_push(x, z, r_af.at[0, 0], to_zf)
    a_push(x, z, r_ab.at[0, 0], to_zb)
    b_push(x, z, r_bx.at[0, 0], to_xf)
    b_push(x, z, r_bx.at[1, 0], to_xb)
    spread_half(0)
    spread_half(1)
    for h in range(2):
        spread[h][vir] = sent[h][vir]

    a_wait(xb, z, r_ax.at[0])
    a_push(xb, z, r_ax.at[2], to_xf)
    a_push(xb, z, r_af.at[0, 1], to_zf)
    a_push(xb, z, r_ab.at[0, 1], to_zb)
    a_wait(xf, z, r_ax.at[1])
    a_push(xf, z, r_af.at[0, 2], to_zf)
    a_push(xf, z, r_ab.at[0, 2], to_zb)
    b_wait(xb, z, r_bx.at[0, 0])
    b_push(xb, z, r_bx.at[2, 0], to_xf)
    prepare(x, z, 0, BLOCKS)
    prepare(xb, z, 0, BLOCKS)
    a_wait(xo, z, r_ax.at[2])
    a_push(xo, z, r_af.at[0, 3], to_zf)
    a_push(xo, z, r_ab.at[0, 3], to_zb)

    def own_rest():
        b_wait(xf, z, r_bx.at[1, 0])
        prepare(xf, z, 0, BLOCKS)
        b_wait(xo, z, r_bx.at[2, 0])
        prepare(xo, z, 0, BLOCKS)

    def ways(s):
        yield (z - sign * (s + 1) + Z) % Z, r_af, r_bf, s + 1, FWD, to_zf
        yield (z + sign * (s + 1) + Z) % Z, r_ab, r_bb, s + 1 + FWD, BWD, to_zb

    def both(s, last=False):
        return list(ways(s))[: 1 if last else 2]

    def ring(s, final=0):
        way = both(s, final == 2)
        goes = (final < 2, final < 1)
        for (zz, r_a, r_b, q, _, to), go in zip(way, goes):
            b_wait(x, zz, r_b.at[s])
            if go:
                b_push(x, zz, r_b.at[s + 1], to)
            b_push(x, zz, r_bx.at[0, q], to_xf)
            b_push(x, zz, r_bx.at[1, q], to_xb)
        for i in range(X):
            for (zz, r_a, r_b, q, _, to), go in zip(way, goes):
                a_wait(xs[i], zz, r_a.at[s, i])
                if go:
                    a_push(xs[i], zz, r_a.at[s + 1, i], to)

    def settle(s, last=False):
        for zz, *_ in both(s, last):
            prepare(x, zz, 0, BLOCKS)
            for i in range(1, X):
                prepare(xs[i], zz, 0, NA)

    def pass_on(s, last=False):
        for zz, _, _, q, _, _ in both(s, last):
            b_wait(xb, zz, r_bx.at[0, q])
            b_push(xb, zz, r_bx.at[2, q], to_xf)

    def near(s, last=False):
        for zz, _, _, q, _, _ in both(s, last):
            prepare(xb, zz, NA, BLOCKS)
            b_wait(xf, zz, r_bx.at[1, q])
            prepare(xf, zz, NA, BLOCKS)

    def far(s, last=False):
        for zz, _, _, q, _, _ in both(s, last):
            b_wait(xo, zz, r_bx.at[2, q])
            prepare(xo, zz, NA, BLOCKS)

    def step(s, final=0):
        ring(s, final)
        pass_on(s - 1)
        settle(s, final == 2)
        near(s - 1)
        far(s - 2)

    def gather_amps(h):
        many = spread[h].at[pl.ds(0, V - 1)]
        pltpu.make_async_copy(many, many, r_y2.at[h]).wait()
        value = abuf[h]
        high = value.astype(jnp.bfloat16)
        cols = slice(HALF * h, HALF * h + HALF)
        aa[:OCC, cols] = high
        aa[OCC:, cols] = (value - high.astype(jnp.float32)).astype(jnp.bfloat16)

    def multiply(xx):
        span = Z * ROWS
        rows = pl.ds(pl.multiple_of(xx * span, span), span)
        right = aa[...]
        dims = (((1,), (1,)), ((), ()))
        part = lax.dot_general(ehi[rows, :], right, dims, preferred_element_type=jnp.float32)
        part += lax.dot_general(elo[rows, :], right, dims, preferred_element_type=jnp.float32)
        ladder = part[:, :OCC] + part[:, OCC:]
        for b in range(span // 128):
            here = pl.ds(xx * (span // 128) + b, OCC, stride=BLOCKS)
            out[here, :] = base[here, :] + ladder[128 * b : 128 * b + 128].T

    ring(0)
    own_rest()
    settle(0)
    ring(1)
    pass_on(0)
    settle(1)
    near(0)
    step(2)
    return_half(0)

    def body(s, _):
        step(s)
        return 0

    lax.fori_loop(3, 5, body, 0)
    return_half(1)
    step(5)
    step(6, 1)
    gather_amps(0)
    step(7, 2)
    pass_on(7, True)
    gather_amps(1)
    load_resid.wait()
    multiply(x)
    near(7, True)
    far(6)
    multiply(xb)
    multiply(xf)
    far(7, True)
    multiply(xo)

    a_all = raw.at[pl.ds(0, SHARDS - 1), :, pl.ds(0, WA)]
    pltpu.make_async_copy(a_all, a_all, s_a.at[0]).wait()
    b_all = raw.at[pl.ds(0, SHARDS - 1), :, pl.ds(WA, WB)]
    pltpu.make_async_copy(b_all, b_all, s_b.at[0]).wait()
    for phase in range(2):
        for h in range(2):
            many = spread[h].at[pl.ds(0, V - 1)]
            pltpu.make_async_copy(many, many, s_y.at[phase, h]).wait()


def solution(mesh):
    def shards(amps, resid, ints, tasks, pair_tiles, irreps):
        smem = pl.BlockSpec(memory_space=pltpu.SMEM)
        hbm = pl.BlockSpec(memory_space=pl.ANY)
        dma = pltpu.SemaphoreType.DMA
        f32, bf16 = jnp.float32, jnp.bfloat16
        flat = (OCC * BLOCKS, 128)
        total = pl.pallas_call(
            kernel,
            out_shape=jax.ShapeDtypeStruct(flat, f32),
            in_specs=[smem, smem, smem, hbm, hbm, hbm],
            out_specs=pl.BlockSpec(memory_space=pltpu.VMEM),
            scratch_shapes=[
                pltpu.VMEM((SHARDS, ROWS, COLS), f32),
                pltpu.VMEM((COLS, COLS), bf16),
                pltpu.VMEM((COLS, COLS), bf16),
                pltpu.VMEM(flat, f32),
                pltpu.VMEM((V, SHARE, HALF), f32),
                pltpu.VMEM((V, SHARE, HALF), f32),
                pltpu.VMEM((V, SHARE, HALF), f32),
                pltpu.VMEM((V, SHARE, HALF), f32),
                pltpu.VMEM((2, V, SHARE, HALF), f32),
                pltpu.VMEM((2, OCC, HALF), f32),
                pltpu.VMEM((2 * OCC, COLS), bf16),
                pltpu.VMEM(flat, f32),
                pltpu.VMEM((2, ROWS, 128), jnp.int32),
                pltpu.VMEM((1, COLS), jnp.int32),
                dma((3,)),
                dma((1,)),
                dma((1,)),
                dma((2, 2)),
                dma((3,)),
                dma((FWD, X)),
                dma((BWD, X)),
                dma((FWD,)),
                dma((BWD,)),
                dma((3, Z)),
                dma((2,)),
                dma((2,)),
            ],
            compiler_params=pltpu.CompilerParams(collective_id=0, has_side_effects=True),
            name="ladder",
        )(tasks, pair_tiles.T, irreps, amps.reshape(flat), resid.reshape(flat), ints.reshape(ROWS, COLS))
        return total.reshape(OCC, 1, COLS)

    in_specs = (P("occ", "vir", None), P("occ", "vir", None), P("vir", "occ", None), P(), P(), P())
    return jax.shard_map(
        shards, mesh=mesh, in_specs=in_specs, out_specs=P("occ", "vir", None), check_vma=False
    )
```

time: 187 us -> 65.3 us (0.35)
  the two profiles are of different devices: /device:TPU:56 before, /device:TPU:8 now
where the time goes in v1:
time: 65.3 us; the launch traced here: 65 us
  Pallas kernels  63.1 us (97%)
  local copies, waits for them, and re-layouts  1.87 us (3%)
    pallas_call x1, Pallas kernels, shards(): pl.pallas_call(kernel, out_shape=jax.ShapeDtypeStruct(flat, f32), in_spec...  63.1 us
    unnamed x1, local copies, waits for them, and re-layouts  1.87 us

profile of v1, /device:TPU:8, one launch (start us, length us, event | category | flops | bytes accessed | tf_op | source)
XLA Modules:
  0.0 65.0 jit_solution(5472336572829930199)
XLA Ops:
  0.0 63.1 %ladder.1 = f32[1024,128]{1,0:T(8,128)} custom-call(s32[16]{0:T(128)} %tasks.1, s32[2,16]{1,0:T(2,128)} %bitcast.9, s32[19,32]{1,0:T(8,128)} %irr.1, f32[1024,128]{1,0:T(8,128)} %bitcast.6, f32[1024,128]{1,0:T(8,128)} %bitcast.7, f32[16,1024]{1,0:T(8,128)} %bitcast.8), custom_call_target="tpu_custom_call" | custom-call | tf_op jit(solution)/shard_map/ladder/pallas_call | solution.py:311
  63.2 1.9 %copy.9 = f32[128,1,1024]{2,1,0:T(1,128)} copy(f32[128,1,1024]{2,1,0:T(1,128)} %bitcast.5) | data formatting | bytes 1048576

commit v2 on v1

v2 whole, which is shorter than its diff:
```python
import jax
import jax.numpy as jnp
from jax import lax
from jax.experimental import pallas as pl
from jax.experimental.pallas import tpu as pltpu
from jax.sharding import PartitionSpec as P

MESH = pl.DeviceIdType.MESH
X, Z, V = 4, 16, 16
SHARDS = X * Z
ROWS = 16
TILE = 32
COLS = 1024
BLOCKS = COLS // 128
NA = 2
WA = NA * 128
WB = COLS - WA
OCC = 128
SHARE = OCC // V
HALF = COLS // 2
FWD, BWD = Z // 2, Z // 2 - 1
HUB = V // 2


def kernel(
    tasks, pairs, irr, amps, resid, ints, out,
    raw, ehi, elo, whole, sent0, sent1, spread0, spread1, picked, abuf, aa, base, col_key, cd_key,
    s_loc, s_a, s_b, s_y, r_ax, r_af, r_ab, r_bf, r_bb, r_bx, r_y1, r_y2,
):
    occ, vir = lax.axis_index("occ"), lax.axis_index("vir")
    x, z = occ // Z, occ % Z
    sign = 1 - 2 * (vir % 2)
    xf, xb = (x + sign + X) % X, (x - sign + X) % X
    xo = (x + 2) % X
    zf, zb = (z + sign + Z) % Z, (z - sign + Z) % Z
    to_xf, to_xb = (xf * Z + z, vir), (xb * Z + z, vir)
    to_zf, to_zb = (x * Z + zf, vir), (x * Z + zb, vir)
    to_zf2 = (x * Z + (z + 2 * sign + Z) % Z, vir)
    to_zb2 = (x * Z + (z - 2 * sign + Z) % Z, vir)

    sent, spread = (sent0, sent1), (spread0, spread1)
    load_amps = pltpu.make_async_copy(amps, whole, s_loc.at[1])
    load_amps.start()
    load_ints = pltpu.make_async_copy(ints, raw.at[occ], s_loc.at[0])
    load_ints.start()
    load_resid = pltpu.make_async_copy(resid, base, s_loc.at[2])
    load_resid.start()

    barrier = pltpu.get_barrier_semaphore()
    for who in (to_xf, to_xb, to_zf, to_zb, to_zf2, to_zb2):
        pl.semaphore_signal(barrier, inc=1, device_id=who, device_id_type=MESH)

    is_hub = vir == HUB

    @pl.when(is_hub)
    def _():
        pl.semaphore_wait(barrier, 6 + V - 1)

        def tell(m, _):
            peer = (occ, (vir + m) % V)
            pl.semaphore_signal(barrier, inc=1, device_id=peer, device_id_type=MESH)
            return 0

        lax.fori_loop(1, V, tell, 0)

    @pl.when(jnp.logical_not(is_hub))
    def _():
        pl.semaphore_wait(barrier, 6)
        pl.semaphore_signal(barrier, inc=1, device_id=(occ, HUB), device_id_type=MESH)

    load_ints.wait()

    def peer_at(i):
        return (vir + V // 2 + ((i + 1) // 2) * (1 - 2 * (i % 2)) + V) % V

    def spread_half(h):
        def send(i, _):
            peer = peer_at(i)
            pltpu.make_async_remote_copy(
                sent[h].at[peer], spread[h].at[vir],
                s_y.at[0, h], r_y1.at[h], device_id=(occ, peer), device_id_type=MESH,
            ).start()
            return 0

        lax.fori_loop(0, V - 1, send, 0)

    own_rows = pl.ds(pl.multiple_of(SHARE * vir, SHARE), SHARE)

    def return_half(h):
        many = spread[h].at[pl.ds(0, V - 1)]
        pltpu.make_async_copy(many, many, r_y1.at[h]).wait()
        for k in range(V):
            picked[h, k] = spread[h][tasks[k]]
        abuf[h, own_rows] = picked[h, vir]

        def send(i, _):
            peer = peer_at(i)
            pltpu.make_async_remote_copy(
                picked.at[h, peer], abuf.at[h, own_rows],
                s_y.at[1, h], r_y2.at[h], device_id=(occ, peer), device_id_type=MESH,
            ).start()
            return 0

        lax.fori_loop(0, V - 1, send, 0)

    def a_part(xx, zz):
        return raw.at[xx * Z + zz, :, pl.ds(0, WA)]

    def b_part(xx, zz):
        return raw.at[xx * Z + zz, :, pl.ds(WA, WB)]

    def push(part, send_sem, recv_sem, who):
        return pltpu.make_async_remote_copy(
            part, part, send_sem, recv_sem, device_id=who, device_id_type=MESH
        )

    def a_push(xx, zz, recv_sem, who):
        push(a_part(xx, zz), s_a.at[0], recv_sem, who).start()

    def b_push(xx, zz, recv_sem, who):
        push(b_part(xx, zz), s_b.at[0], recv_sem, who).start()

    def a_wait(xx, zz, recv_sem):
        push(a_part(xx, zz), s_a.at[0], recv_sem, to_xf).wait_recv()

    def b_wait(xx, zz, recv_sem):
        push(b_part(xx, zz), s_b.at[0], recv_sem, to_xf).wait_recv()

    xs = (x, xb, xf, xo)

    def prepare(xx, zz, first, last):
        shard = xx * Z + zz
        key = col_key[shard % 2] ^ irr[tile_a, shard // 2]
        rows = pl.ds(pl.multiple_of(shard * ROWS, ROWS), ROWS)
        cols = slice(128 * first, 128 * last)
        keys = jnp.concatenate([key] * (last - first), axis=1)
        value = jnp.where(keys == cd_key[:, cols], raw[shard, :, cols], 0.0)
        high = value.astype(jnp.bfloat16)
        ehi[rows, cols] = high
        elo[rows, cols] = (value - high.astype(jnp.float32)).astype(jnp.bfloat16)

    ways = (
        (sign, FWD, r_af, r_bf, 0, to_zf, to_zf2),
        (-sign, BWD, r_ab, r_bb, FWD, to_zb, to_zb2),
    )

    def along(t):
        for d in (2 * t + 2, 2 * t + 1):
            for way in ways:
                if d <= way[1]:
                    yield d, (z - way[0] * d + Z) % Z, way

    def a_relay(i, d, zz, way):
        _, reach, r_a, _, _, to1, to2 = way
        if d + 2 <= reach:
            a_push(xs[i], zz, r_a.at[d + 1, i], to2)
        if d + 1 <= reach:
            a_push(xs[i], zz, r_a.at[d, i], to1)

    def b_relay(d, zz, way):
        _, reach, _, r_b, _, to1, to2 = way
        if d + 2 <= reach:
            b_push(x, zz, r_b.at[d + 1], to2)
        if d + 1 <= reach:
            b_push(x, zz, r_b.at[d], to1)

    def a_start(i):
        for way in ways:
            a_relay(i, 0, z, way)

    def stage_b(t):
        for d, zz, way in along(t):
            b_wait(x, zz, way[3].at[d - 1])
            if d % 2 == 0:
                b_relay(d, zz, way)
            b_push(x, zz, r_bx.at[0, way[4] + d], to_xf)
            b_push(x, zz, r_bx.at[1, way[4] + d], to_xb)

    def stage_a(t, i):
        for d, zz, way in along(t):
            if d % 2 == 0:
                a_wait(xs[i], zz, way[2].at[d - 1, i])
                a_relay(i, d, zz, way)

    def settle_a(t, i):
        for d, zz, way in along(t):
            if d % 2 == 1:
                a_wait(xs[i], zz, way[2].at[d - 1, i])
            prepare(xs[i], zz, 0, NA)

    def settle_b(t):
        for d, zz, way in along(t):
            prepare(x, zz, NA, BLOCKS)

    def pass_on(t):
        for d, zz, way in along(t):
            q = way[4] + d
            if d % 2 == 0:
                b_wait(xb, zz, r_bx.at[0, q])
                b_push(xb, zz, r_bx.at[2, q], to_xf)
            else:
                b_wait(xf, zz, r_bx.at[1, q])
                b_push(xf, zz, r_bx.at[2, q], to_xb)

    def near(t):
        for d, zz, way in along(t):
            q = way[4] + d
            if d % 2 == 0:
                b_wait(xf, zz, r_bx.at[1, q])
            else:
                b_wait(xb, zz, r_bx.at[0, q])
            prepare(xb, zz, NA, BLOCKS)
            prepare(xf, zz, NA, BLOCKS)

    def far(t):
        for d, zz, way in along(t):
            q = way[4] + d
            b_wait(xo, zz, r_bx.at[2, q])
            prepare(xo, zz, NA, BLOCKS)

    for way in ways:
        b_relay(0, z, way)
    a_push(x, z, r_ax.at[0], to_xf)
    a_push(x, z, r_ax.at[1], to_xb)
    a_start(0)
    b_push(x, z, r_bx.at[0, 0], to_xf)
    b_push(x, z, r_bx.at[1, 0], to_xb)
    load_amps.wait()

    def arrange(j, _):
        for b in range(BLOCKS):
            block = whole[pl.ds(SHARE * BLOCKS * j + b, SHARE, stride=BLOCKS), :]
            col = 128 * b % HALF
            sent[128 * b // HALF][j, :, col : col + 128] = block
        return 0

    lax.fori_loop(0, V, arrange, 0)
    for h in range(2):
        spread[h][vir] = sent[h][vir]

    tile_a, tile_b = pairs[0, vir], pairs[1, vir]
    task = tasks[vir]
    cd_a, cd_b = pairs[0, task], pairs[1, task]
    sub = lax.broadcasted_iota(jnp.int32, (ROWS, 128), 0)
    for par in range(2):
        key = jnp.zeros((ROWS, 128), jnp.int32)
        for j in range(ROWS):
            key = jnp.where(sub == j, irr[tile_b, par * ROWS + j], key)
        col_key[par] = key
    lane = lax.broadcasted_iota(jnp.int32, (1, 128), 1)
    minor = jnp.zeros((1, 128), jnp.int32)
    for j in range(TILE):
        minor = jnp.where(lane % TILE == j, irr[cd_b, j], minor)
    for b in range(BLOCKS):
        major = jnp.zeros((1, 128), jnp.int32)
        for j in range(4):
            major = jnp.where(lane // TILE == j, irr[cd_a, 4 * b + j], major)
        cd_key[:, 128 * b : 128 * b + 128] = major ^ minor

    prepare(x, z, 0, BLOCKS)

    a_wait(xb, z, r_ax.at[0])
    a_push(xb, z, r_ax.at[2], to_xf)
    a_start(1)
    a_wait(xf, z, r_ax.at[1])
    a_start(2)
    b_wait(xb, z, r_bx.at[0, 0])
    b_push(xb, z, r_bx.at[2, 0], to_xf)
    @pl.when(jnp.logical_not(is_hub))
    def _():
        pl.semaphore_wait(barrier, 1)

    spread_half(0)
    spread_half(1)
    prepare(xb, z, 0, BLOCKS)
    stage_b(0)
    stage_a(0, 0)
    a_wait(xo, z, r_ax.at[2])
    a_start(3)
    b_wait(xf, z, r_bx.at[1, 0])
    prepare(xf, z, 0, BLOCKS)

    def gather_amps(h):
        many = spread[h].at[pl.ds(0, V - 1)]
        pltpu.make_async_copy(many, many, r_y2.at[h]).wait()
        value = abuf[h]
        high = value.astype(jnp.bfloat16)
        cols = slice(HALF * h, HALF * h + HALF)
        aa[:OCC, cols] = high
        aa[OCC:, cols] = (value - high.astype(jnp.float32)).astype(jnp.bfloat16)

    def multiply(xx):
        span = Z * ROWS
        rows = pl.ds(pl.multiple_of(xx * span, span), span)
        right = aa[...]
        dims = (((1,), (1,)), ((), ()))
        part = lax.dot_general(ehi[rows, :], right, dims, preferred_element_type=jnp.float32)
        part += lax.dot_general(elo[rows, :], right, dims, preferred_element_type=jnp.float32)
        ladder = part[:, :OCC] + part[:, OCC:]
        for b in range(span // 128):
            here = pl.ds(xx * (span // 128) + b, OCC, stride=BLOCKS)
            out[here, :] = base[here, :] + ladder[128 * b : 128 * b + 128].T

    def later_a(t):
        stage_a(t, 1)
        stage_a(t, 2)
        settle_a(t, 0)

    def last_a(t):
        stage_a(t, 3)
        settle_b(t)
        settle_a(t, 1)
        settle_a(t, 2)

    later_a(0)
    stage_b(1)
    stage_a(1, 0)
    pass_on(0)
    last_a(0)
    b_wait(xo, z, r_bx.at[2, 0])
    prepare(xo, z, 0, BLOCKS)
    later_a(1)
    return_half(0)
    stage_b(2)
    stage_a(2, 0)
    pass_on(1)
    last_a(1)
    settle_a(0, 3)
    near(0)
    return_half(1)
    later_a(2)
    stage_b(3)
    stage_a(3, 0)
    pass_on(2)
    last_a(2)
    settle_a(1, 3)
    far(0)
    near(1)
    later_a(3)
    pass_on(3)
    last_a(3)
    settle_a(2, 3)
    far(1)
    near(2)
    settle_a(3, 3)
    far(2)
    gather_amps(0)
    gather_amps(1)
    load_resid.wait()
    multiply(x)
    near(3)
    multiply(xb)
    multiply(xf)
    far(3)
    multiply(xo)

    a_all = raw.at[pl.ds(0, SHARDS - 1), :, pl.ds(0, WA)]
    pltpu.make_async_copy(a_all, a_all, s_a.at[0]).wait()
    b_all = raw.at[pl.ds(0, SHARDS - 1), :, pl.ds(WA, WB)]
    pltpu.make_async_copy(b_all, b_all, s_b.at[0]).wait()
    for phase in range(2):
        for h in range(2):
            many = spread[h].at[pl.ds(0, V - 1)]
            pltpu.make_async_copy(many, many, s_y.at[phase, h]).wait()


def solution(mesh):
    def shards(amps, resid, ints, tasks, pair_tiles, irreps):
        smem = pl.BlockSpec(memory_space=pltpu.SMEM)
        hbm = pl.BlockSpec(memory_space=pl.ANY)
        dma = pltpu.SemaphoreType.DMA
        f32, bf16 = jnp.float32, jnp.bfloat16
        flat = (OCC * BLOCKS, 128)
        total = pl.pallas_call(
            kernel,
            out_shape=jax.ShapeDtypeStruct(flat, f32),
            in_specs=[smem, smem, smem, hbm, hbm, hbm],
            out_specs=pl.BlockSpec(memory_space=pltpu.VMEM),
            scratch_shapes=[
                pltpu.VMEM((SHARDS, ROWS, COLS), f32),
                pltpu.VMEM((COLS, COLS), bf16),
                pltpu.VMEM((COLS, COLS), bf16),
                pltpu.VMEM(flat, f32),
                pltpu.VMEM((V, SHARE, HALF), f32),
                pltpu.VMEM((V, SHARE, HALF), f32),
                pltpu.VMEM((V, SHARE, HALF), f32),
                pltpu.VMEM((V, SHARE, HALF), f32),
                pltpu.VMEM((2, V, SHARE, HALF), f32),
                pltpu.VMEM((2, OCC, HALF), f32),
                pltpu.VMEM((2 * OCC, COLS), bf16),
                pltpu.VMEM(flat, f32),
                pltpu.VMEM((2, ROWS, 128), jnp.int32),
                pltpu.VMEM((1, COLS), jnp.int32),
                dma((3,)),
                dma((1,)),
                dma((1,)),
                dma((2, 2)),
                dma((3,)),
                dma((FWD, X)),
                dma((BWD, X)),
                dma((FWD,)),
                dma((BWD,)),
                dma((3, Z)),
                dma((2,)),
                dma((2,)),
            ],
            compiler_params=pltpu.CompilerParams(collective_id=0, has_side_effects=True),
            name="ladder",
        )(tasks, pair_tiles.T, irreps, amps.reshape(flat), resid.reshape(flat), ints.reshape(ROWS, COLS))
        return total.reshape(OCC, 1, COLS)

    in_specs = (P("occ", "vir", None), P("occ", "vir", None), P("vir", "occ", None), P(), P(), P())
    return jax.shard_map(
        shards, mesh=mesh, in_specs=in_specs, out_specs=P("occ", "vir", None), check_vma=False
    )
```

time: 65.3 us -> 59.2 us (0.907)
  Pallas kernels: 63.1 us -> 57.1 us
    pallas_call x1, Pallas kernels: 63.1 us -> 57.1 us  [shards(): pl.pallas_call(kernel, out_shape=jax.ShapeDtypeStruct(flat, f32), in_spec...]
where the time goes in v2:
time: 59.2 us; the launch traced here: 59 us
  Pallas kernels  57.1 us (96%)
  local copies, waits for them, and re-layouts  1.87 us (3%)
    pallas_call x1, Pallas kernels, shards(): pl.pallas_call(kernel, out_shape=jax.ShapeDtypeStruct(flat, f32), in_spec...  57.1 us
    unnamed x1, local copies, waits for them, and re-layouts  1.87 us

profile of v2, /device:TPU:8, one launch (start us, length us, event | category | flops | bytes accessed | tf_op | source)
XLA Modules:
  0.0 59.0 jit_solution(7738544312512653815)
XLA Ops:
  0.0 57.1 %ladder.1 = f32[1024,128]{1,0:T(8,128)} custom-call(s32[16]{0:T(128)} %tasks.1, s32[2,16]{1,0:T(2,128)} %bitcast.9, s32[19,32]{1,0:T(8,128)} %irr.1, f32[1024,128]{1,0:T(8,128)} %bitcast.6, f32[1024,128]{1,0:T(8,128)} %bitcast.7, f32[16,1024]{1,0:T(8,128)} %bitcast.8), custom_call_target="tpu_custom_call" | custom-call | tf_op jit(solution)/shard_map/ladder/pallas_call | solution.py:374
  57.1 1.9 %copy.9 = f32[128,1,1024]{2,1,0:T(1,128)} copy(f32[128,1,1024]{2,1,0:T(1,128)} %bitcast.5) | data formatting | bytes 1048576

commit v3 on v2

--- a/solution.py
+++ b/solution.py
@@ -19,6 +19,7 @@
 SHARE = OCC // V
 HALF = COLS // 2
 FWD, BWD = Z // 2, Z // 2 - 1
+LAST = FWD // 2 - 1
 HUB = V // 2
 
 
@@ -35,6 +36,7 @@
     zf, zb = (z + sign + Z) % Z, (z - sign + Z) % Z
     to_xf, to_xb = (xf * Z + z, vir), (xb * Z + z, vir)
     to_zf, to_zb = (x * Z + zf, vir), (x * Z + zb, vir)
+    to_xo = (xo * Z + z, vir)
     to_zf2 = (x * Z + (z + 2 * sign + Z) % Z, vir)
     to_zb2 = (x * Z + (z - 2 * sign + Z) % Z, vir)
 
@@ -47,14 +49,15 @@
     load_resid.start()
 
     barrier = pltpu.get_barrier_semaphore()
-    for who in (to_xf, to_xb, to_zf, to_zb, to_zf2, to_zb2):
+    near_by = (to_xf, to_xb, to_xo, to_zf, to_zb, to_zf2, to_zb2)
+    for who in near_by:
         pl.semaphore_signal(barrier, inc=1, device_id=who, device_id_type=MESH)
 
     is_hub = vir == HUB
 
     @pl.when(is_hub)
     def _():
-        pl.semaphore_wait(barrier, 6 + V - 1)
+        pl.semaphore_wait(barrier, len(near_by) + V - 1)
 
         def tell(m, _):
             peer = (occ, (vir + m) % V)
@@ -65,7 +68,7 @@
 
     @pl.when(jnp.logical_not(is_hub))
     def _():
-        pl.semaphore_wait(barrier, 6)
+        pl.semaphore_wait(barrier, len(near_by))
         pl.semaphore_signal(barrier, inc=1, device_id=(occ, HUB), device_id_type=MESH)
 
     load_ints.wait()
@@ -175,6 +178,8 @@
                 b_relay(d, zz, way)
             b_push(x, zz, r_bx.at[0, way[4] + d], to_xf)
             b_push(x, zz, r_bx.at[1, way[4] + d], to_xb)
+            if t == LAST:
+                b_push(x, zz, r_bx.at[2, way[4] + d], to_xo)
 
     def stage_a(t, i):
         for d, zz, way in along(t):
@@ -197,10 +202,12 @@
             q = way[4] + d
             if d % 2 == 0:
                 b_wait(xb, zz, r_bx.at[0, q])
-                b_push(xb, zz, r_bx.at[2, q], to_xf)
+                if t < LAST:
+                    b_push(xb, zz, r_bx.at[2, q], to_xf)
             else:
                 b_wait(xf, zz, r_bx.at[1, q])
-                b_push(xf, zz, r_bx.at[2, q], to_xb)
+                if t < LAST:
+                    b_push(xf, zz, r_bx.at[2, q], to_xb)
 
     def near(t):
         for d, zz, way in along(t):
@@ -222,6 +229,7 @@
         b_relay(0, z, way)
     a_push(x, z, r_ax.at[0], to_xf)
     a_push(x, z, r_ax.at[1], to_xb)
+    a_push(x, z, r_ax.at[2], to_xo)
     a_start(0)
     b_push(x, z, r_bx.at[0, 0], to_xf)
     b_push(x, z, r_bx.at[1, 0], to_xb)
@@ -260,7 +268,6 @@
     prepare(x, z, 0, BLOCKS)
 
     a_wait(xb, z, r_ax.at[0])
-    a_push(xb, z, r_ax.at[2], to_xf)
     a_start(1)
     a_wait(xf, z, r_ax.at[1])
     a_start(2)

time: 59.2 us -> 61.1 us (1.032)
  the two profiles are of different devices: /device:TPU:8 before, /device:TPU:2 now
where the time goes in v3:
time: 61.1 us; the launch traced here: 60.8 us
  Pallas kernels  59 us (97%)
  local copies, waits for them, and re-layouts  1.87 us (3%)
    pallas_call x1, Pallas kernels, shards(): pl.pallas_call(kernel, out_shape=jax.ShapeDtypeStruct(flat, f32), in_spec...  59 us
    unnamed x1, local copies, waits for them, and re-layouts  1.87 us

profile of v3, /device:TPU:2, one launch (start us, length us, event | category | flops | bytes accessed | tf_op | source)
XLA Modules:
  0.0 60.8 jit_solution(2132284542852922812)
XLA Ops:
  0.0 59.0 %ladder.1 = f32[1024,128]{1,0:T(8,128)} custom-call(s32[16]{0:T(128)} %tasks.1, s32[2,16]{1,0:T(2,128)} %bitcast.9, s32[19,32]{1,0:T(8,128)} %irr.1, f32[1024,128]{1,0:T(8,128)} %bitcast.6, f32[1024,128]{1,0:T(8,128)} %bitcast.7, f32[16,1024]{1,0:T(8,128)} %bitcast.8), custom_call_target="tpu_custom_call" | custom-call | tf_op jit(solution)/shard_map/ladder/pallas_call | solution.py:381
  59.0 1.9 %copy.9 = f32[128,1,1024]{2,1,0:T(1,128)} copy(f32[128,1,1024]{2,1,0:T(1,128)} %bitcast.5) | data formatting | bytes 1048576
